TPU v7x, 32 devices: a whole 2x2x4 slice. The times are simulated.
32 devices in a mesh: tile: 8 (over z, y), grp: 4 (over x, core).
Axes of the slice: x: 2, y: 2, z: 4, core: 2. Of those that a mesh axis runs over, the one named last changes fastest.
Arguments:
- left_triples: bfloat16 [256, 6144, 300], P('tile', 'grp'), may hold values from -6 to 6
- right_triples: bfloat16 [256, 6144, 300], P('tile', 'grp'), may hold values from -6 to 6
- live_tiles: int32 [256, 24], P('tile', 'grp'), may hold values from 0 to 1
- vv_block: bfloat16 [300, 300], replicated, may hold values from -0.375 to 0.375
- slab_block: bfloat16 [256, 256], replicated, may hold values from -0.375 to 0.375
- left_doubles: bfloat16 [256, 8192], P('tile', 'grp'), may hold values from -6 to 6
- ov_block: bfloat16 [30, 300], replicated, may hold values from -6 to 6
- pair_index: int32 [6144], P('grp'), may hold values from 0 to 8191
- occ_index: int32 [6144], P('grp'), may hold values from 0 to 29
Outputs:
- sigma_out: bfloat16 [256, 6144, 300], P('tile', 'grp')
- density: float32 [300, 300], replicated
All inputs are finite; a program needn't handle non-finite values.
Results may differ from a plain program's by a relative error of at most 0.0026.
Values may be sent and summed in bfloat16 or wider, within the bound.
No kernel may reach another device: no remote copies, remote signals or barrier semaphores. Data moves between devices by JAX's collectives and lax.ppermute only.
A program may use at most 320 MiB of HBM per device.

v0:
```python
import math
import jax
import jax.numpy as jnp
from jax import lax
from jax.sharding import PartitionSpec as P


def body(
    left_triples,
    right_triples,
    live_tiles,
    vv_block,
    slab_block,
    left_doubles,
    ov_block,
    pair_index,
    occ_index,
):
    slab_count, row_count, feature = left_triples.shape
    tile_count = live_tiles.shape[1]
    tile_rows = row_count // tile_count
    live_mask = live_tiles.astype(jnp.bfloat16)
    masked = (
        left_triples.reshape(slab_count, tile_count, tile_rows, feature)
        * live_mask[:, :, None, None]
    ).reshape(slab_count, row_count, feature)
    mixed_rows = jnp.einsum(
        "bd,drc->brc",
        slab_block,
        lax.all_to_all(masked, "tile", split_axis=1, concat_axis=0, tiled=True),
        preferred_element_type=jnp.float32,
    ).astype(jnp.bfloat16)
    slab_term = lax.all_to_all(mixed_rows, "tile", split_axis=0, concat_axis=1, tiled=True)
    full_table = lax.all_gather(left_doubles, "grp", axis=1, tiled=True)
    picked = jnp.take(full_table, pair_index, axis=1).astype(jnp.float32)
    onehot = (occ_index[:, None] == jnp.arange(ov_block.shape[0], dtype=jnp.int32)[None, :]).astype(
        jnp.bfloat16
    )
    occ_rows = jnp.dot(onehot, ov_block, preferred_element_type=jnp.float32)
    pair_term = picked[:, :, None] * occ_rows[None, :, :]
    flat_rows = masked.reshape(-1, feature)
    vv_term = jnp.dot(flat_rows, vv_block, preferred_element_type=jnp.float32).reshape(
        slab_count, row_count, feature
    )
    partial_value = lax.dot_general(
        flat_rows,
        right_triples.reshape(-1, feature),
        (((0,), (0,)), ((), ())),
        preferred_element_type=jnp.float32,
    )
    summed = vv_term + slab_term.astype(jnp.float32) + pair_term
    summed = (
        summed.reshape(slab_count, tile_count, tile_rows, feature)
        * live_tiles.astype(jnp.float32)[:, :, None, None]
    )
    sigma_out = summed.reshape(slab_count, row_count, feature).astype(jnp.bfloat16)
    norm_scale = math.sqrt(slab_count * lax.axis_size("tile") * row_count * lax.axis_size("grp"))
    density = lax.psum(partial_value, ("tile", "grp")) / norm_scale
    return (sigma_out, density)


def solution(mesh):
    in_specs = (
        P("tile", "grp", None),
        P("tile", "grp", None),
        P("tile", "grp"),
        P(),
        P(),
        P("tile", "grp"),
        P(),
        P("grp"),
        P("grp"),
    )
    out_specs = (P("tile", "grp", None), P())
    return jax.shard_map(body, mesh=mesh, in_specs=in_specs, out_specs=out_specs, check_vma=False)
```

profile of v0, /device:TPU:0, one launch (start us, length us, event | category | flops | bytes accessed | tf_op | source)
XLA Modules:
  0.0 2170.5 jit_solution(17723983579102497324)
XLA Ops:
  7.2 0.0 copy-start
  7.2 1.4 fusion.17
  8.5 0.1 copy.70
  8.6 0.1 mul.42
  8.8 20.2 broadcast_multiply_fusion
  28.9 48.6 %copy.73 = bf16[32,1536,300]{2,0,1:T(8,128)(2,1)} copy(bf16[32,1536,300]{1,0,2:T(8,128)(2,1)} %broadcast_multiply_fusion) | data formatting | bytes 58982400 | tf_op jit(solution)/shard_map/mul | solution.py:24
  77.6 825.9 %all_to_all.27 = bf16[32,1536,300]{2,0,1:T(8,128)(2,1)} all-to-all(bf16[32,1536,300]{2,0,1:T(8,128)(2,1)} %copy.73), channel_id=1, replica_groups=mesh['tile'=8,'grp'=4] {'tile'}, dimensions={1} | all-to-all | bytes 58982400 | tf_op jit(solution)/shard_map/all_to_all | solution.py:30
  903.5 0.0 copy-start.1
  903.5 25.6 %copy.75 = bf16[8,32,192,300]{3,2,1,0:T(8,128)(2,1)} copy(bf16[8,32,192,300]{3,1,2,0:T(8,128)(2,1)} %bitcast.31) | data formatting | bytes 58982400 | tf_op jit(solution)/shard_map/all_to_all | solution.py:30
  929.1 0.0 copy-done.1
  929.1 38.3 %convert_bitcast_fusion.1 = bf16[256,192,300]{0,2,1:T(8,128)(2,1)} fusion(bf16[256,192,300]{2,1,0:T(8,128)(2,1)} %bitcast.30, bf16[256,256]{1,0:T(8,128)(2,1)S(1)} %copy-done.1), kind=kOutput, calls=%fused_computation.7 | convolution fusion | flops 7564492800 | bytes 59113472 | tf_op jit(solution)/shard_map/bd,drc->brc/dot_general | solution.py:27
  967.4 45.9 %copy.77 = bf16[256,192,300]{2,1,0:T(8,128)(2,1)} copy(bf16[256,192,300]{0,2,1:T(8,128)(2,1)} %convert_bitcast_fusion.1) | data formatting | bytes 58982400 | tf_op jit(solution)/shard_map/convert_element_type | solution.py:32
  1013.2 7.5 all-to-all-start.1
  1020.7 0.0 copy-start.5
  1020.7 0.0 copy-start.2
  1020.7 0.0 copy-start.3
  1020.8 0.0 copy-start.4
  1020.8 0.0 copy-start.6
  1020.8 0.0 all-reduce.2.cloned.1.call-start
  1020.8 71.6 %fusion.8 = f32[300,300]{1,0:T(8,128)} fusion(bf16[32,1536,300]{1,0,2:T(8,128)(2,1)} %param.10, bf16[32,1536,300]{1,0,2:T(8,128)(2,1)} %broadcast_multiply_fusion), kind=kOutput, calls=%fused_computation.11 | convolution fusion | flops 8847360000 | bytes 59342400 | tf_op jit(solution)/shard_map/dot_general | solution.py:45
  1092.4 0.0 all-reduce.2.cloned.1.call-update
  1092.4 0.0 copy-done.5
  1092.4 0.1 copy.82
  1092.5 0.1 mul.49
  1092.6 0.1 copy.93
  1092.7 0.0 copy-done.2
  1092.7 0.3 copy.80
  1093.0 0.0 copy-done.3
  1093.0 16.5 all_gather.3
  1109.5 3.2 gather_fusion
  1112.7 0.3 convert_bitcast_fusion.2
  1113.0 0.2 copy.81
  1113.2 0.0 copy-done.4
  1113.2 0.0 copy-done.6
  1113.2 1.3 fusion.13
  1114.5 787.4 %all-reduce.2.cloned.1.call-done = f32[300,300]{1,0:T(8,128)} async-done(((f32[300,300]{1,0:T(8,128)}), f32[300,300]{1,0:T(8,128)}) %all-reduce.2.cloned.1.call-update) | async-done | bytes 360016 | tf_op jit(solution)/shard_map/psum | solution.py:58
  1901.9 1.8 broadcast_multiply_fusion.1
  1903.8 0.0 all-to-all-done.1
  1903.8 36.0 %convert_bitcast_fusion = f32[32,8,192,300]{3,2,0,1:T(8,128)} fusion(bf16[8,32,192,300]{3,2,1,0:T(8,128)(2,1)} %bitcast.12), kind=kLoop, calls=%fused_computation.1 | loop fusion | flops 14745600 | bytes 88473600 | tf_op jit(solution)/shard_map/convert_element_type | solution.py:51
  1939.8 90.5 %copy.90 = f32[32,8,192,300]{2,1,3,0:T(8,128)} copy(f32[32,8,192,300]{3,2,0,1:T(8,128)} %convert_bitcast_fusion) | data formatting | bytes 117964800 | tf_op jit(solution)/shard_map/convert_element_type | solution.py:51
  2030.3 64.1 %reshape.67 = f32[32,1536,300]{1,2,0:T(8,128)} reshape(f32[32,8,192,300]{2,1,3,0:T(8,128)} %copy.90) | data formatting | bytes 117964800 | tf_op jit(solution)/shard_map/convert_element_type | solution.py:51
  2094.5 0.0 copy-done
  2094.5 48.1 %multiply_convert_fusion = bf16[32,1536,300]{1,2,0:T(8,128)(2,1)} fusion(f32[32,1536,300]{1,2,0:T(8,128)} %reshape.67, f32[32,1536]{1,0:T(8,128)S(1)} %bitcast.32, f32[1536,300]{0,1:T(8,128)S(1)} %fusion.13, f32[32,1536]{1,0:T(8,128)S(1)} %copy.81, bf16[32,1536,300]{1,0,2:T(8,128)(2,1)} %broadcast_multiply_fusion, bf16[300,300]{1,0:T(8,128)(2,1)S(1)} %copy-done), kind=kOutput, calls=%fused_computation.2 | convolution fusion | flops 8921088000 | bytes 120381216 | tf_op jit(solution)/shard_map/dot_general | solution.py:42
  2142.6 20.6 copy.85
  (4 shorter events, 0.0 us)
Async XLA Ops:
  7.2 2087.3 %copy-start = (bf16[300,300]{1,0:T(8,128)(2,1)S(1)}, bf16[300,300]{1,0:T(8,128)(2,1)}, u32[]{:S(2)}) copy-start(bf16[300,300]{1,0:T(8,128)(2,1)} %param.12) | copy-start | bytes 540004
  903.5 25.6 %copy-start.1 = (bf16[256,256]{1,0:T(8,128)(2,1)S(1)}, bf16[256,256]{1,0:T(8,128)(2,1)}, u32[]{:S(2)}) copy-start(bf16[256,256]{1,0:T(8,128)(2,1)} %param.13) | copy-start | bytes 393220
  1013.2 890.5 %all-to-all-start.1 = ((bf16[256,192,300]{2,1,0:T(8,128)(2,1)}), bf16[256,192,300]{2,1,0:T(8,128)(2,1)}, u32[]{:S(2)}, u32[]{:S(2)}) async-start(bf16[256,192,300]{2,1,0:T(8,128)(2,1)} %copy.77), calls=%async_computation.1 | async-start | bytes 75497472 | tf_op jit(solution)/shard_map/all_to_all | solution.py:33
  1020.7 71.7 %copy-start.5 = (f32[32,6]{0,1:T(8,128)S(1)}, f32[32,6]{0,1:T(8,128)}, u32[]{:S(2)}) copy-start(f32[32,6]{0,1:T(8,128)} %get-tuple-element.12) | copy-start | bytes 2308
  1020.7 72.0 %copy-start.2 = (bf16[32,2048]{1,0:T(8,128)(2,1)S(1)}, bf16[32,2048]{1,0:T(8,128)(2,1)}, u32[]{:S(2)}) copy-start(bf16[32,2048]{1,0:T(8,128)(2,1)} %param.14) | copy-start | bytes 393220
  1020.7 72.3 %copy-start.3 = (s32[1536]{0:T(1024)S(1)}, s32[1536]{0:T(1024)}, u32[]{:S(2)}) copy-start(s32[1536]{0:T(1024)} %param.16) | copy-start | bytes 18436
  1020.8 92.5 %copy-start.4 = (bf16[30,300]{1,0:T(8,128)(2,1)S(1)}, bf16[30,300]{1,0:T(8,128)(2,1)}, u32[]{:S(2)}) copy-start(bf16[30,300]{1,0:T(8,128)(2,1)} %param.15) | copy-start | bytes 54004
  1020.8 92.5 %copy-start.6 = (s32[1536]{0:T(1024)S(1)}, s32[1536]{0:T(1024)}, u32[]{:S(2)}) copy-start(s32[1536]{0:T(1024)} %param.17) | copy-start | bytes 18436
  1020.8 881.2 %all-reduce.2.cloned.1.call-start = ((), (), s32[]{:S(2)}) async-start(), calls=%async_computation.2 | async-start | bytes 933888 | tf_op jit(solution)/shard_map/psum | solution.py:58
Sparse Core Ops, SparseCore 0:
  1092.6 809.3 all-reduce.1
where the time goes:
time: 2180 us; the launch traced here: 2170 us
  blocking collectives  842 us (39%)
  waiting for transfers between devices  787 us (36%)
  local copies, waits for them, and re-layouts  300 us (14%)
  matrix products  159 us (7%)
  other arithmetic  59.7 us (3%)
    all_to_all x1, blocking collectives, body(): lax.all_to_all(masked, 'tile', split_axis=1, concat_axis=0, tiled=True)  826 us
    psum x1, waiting for transfers between devices, body(): density = lax.psum(partial_value, ('tile', 'grp')) / norm_scale  787 us
    convert_element_type x2, local copies, waits for them, and re-layouts, body(): summed = vv_term + slab_term.astype(jnp.float32) + pair_term  155 us
    dot_general x1, matrix products, body(): lax.dot_general(flat_rows, right_triples.reshape(-1, feature), (((0,), (0...  71.6 us
    mul x2, local copies, waits for them, and re-layouts, body(): left_triples.reshape(slab_count, tile_count, tile_rows, feature)  48.7 us
    dot_general x1, matrix products, body(): jnp.dot(flat_rows, vv_block, preferred_element_type=jnp.float32)  48.1 us
    convert_element_type x1, local copies, waits for them, and re-layouts, body(): mixed_rows = jnp.einsum('bd,drc->brc', slab_block, lax.all_to_all(masked,...  45.9 us
  transfers between devices with their start and end apart: 2, of which 1 were waited for; matrix products, arithmetic and copies ran while one was open for 4% of the time, Pallas kernels for 0%

commit v1 on v0

--- a/solution.py
+++ b/solution.py
@@ -16,6 +16,19 @@
     pair_index,
     occ_index,
 ):
+
+    def assign_the_lots_all(pos_dim, where_dim, s0):
+        raw_out = jnp.concatenate(
+            lax.all_to_all(
+                jnp.stack(jnp.split(s0, lax.psum(1, "tile"), axis=pos_dim)),
+                "tile",
+                split_axis=0,
+                concat_axis=0,
+            ),
+            axis=where_dim,
+        )
+        return raw_out
+
     slab_count, row_count, feature = left_triples.shape
     tile_count = live_tiles.shape[1]
     tile_rows = row_count // tile_count
@@ -27,7 +40,7 @@
     mixed_rows = jnp.einsum(
         "bd,drc->brc",
         slab_block,
-        lax.all_to_all(masked, "tile", split_axis=1, concat_axis=0, tiled=True),
+        assign_the_lots_all(1, 0, masked),
         preferred_element_type=jnp.float32,
     ).astype(jnp.bfloat16)
     slab_term = lax.all_to_all(mixed_rows, "tile", split_axis=0, concat_axis=1, tiled=True)

time: 2180 us -> 2190 us (level)
  matrix products: 159 us -> 121 us
  waiting for transfers between devices: 787 us -> 822 us
    unnamed x18 -> x26, local copies, waits for them, and re-layouts: 21.1 us -> 99.8 us
    mul x2 -> x1, local copies, waits for them, and re-layouts: 48.7 us -> 0.1 us  [body(): left_triples.reshape(slab_count, tile_count, tile_rows, feature)]
    dot_general x1, matrix products: 71.6 us -> 37 us  [body(): lax.dot_general(flat_rows, right_triples.reshape(-1, feature), (((0,), (0...]
    psum x1, waiting for transfers between devices: 787 us -> 822 us  [body(): density = lax.psum(partial_value, ('tile', 'grp')) / norm_scale]
    all_to_all x1 -> x0, local copies, waits for them, and re-layouts: 25.6 us -> none  [body(): lax.all_to_all(masked, 'tile', split_axis=1, concat_axis=0, tiled=True)]
  transfers between devices with their start and end apart: 2 -> 2, of which waited for: 1 -> 1; matrix products, arithmetic and copies ran while one was open for 4% -> 2% of each run, Pallas kernels for 0% -> 0%
where the time goes in v1:
time: 2190 us; the launch traced here: 2180 us
  blocking collectives  843 us (38%)
  waiting for transfers between devices  822 us (38%)
  local copies, waits for them, and re-layouts  309 us (14%)
  matrix products  121 us (6%)
  other arithmetic  65.1 us (3%)
    all_to_all x1, blocking collectives, assign_the_lots_all(): lax.all_to_all(jnp.stack(jnp.split(s0, lax.psum(1, 'tile'), axis=pos_dim)...  826 us
    psum x1, waiting for transfers between devices, body(): density = lax.psum(partial_value, ('tile', 'grp')) / norm_scale  822 us
    convert_element_type x2, local copies, waits for them, and re-layouts, body(): summed = vv_term + slab_term.astype(jnp.float32) + pair_term  155 us
    unnamed x26, local copies, waits for them, and re-layouts  99.8 us
    convert_element_type x1, local copies, waits for them, and re-layouts, body(): mixed_rows = jnp.einsum('bd,drc->brc', slab_block, assign_the_lots_all(1,...  45.9 us
    dot_general x1, matrix products, body(): jnp.dot(flat_rows, vv_block, preferred_element_type=jnp.float32)  44.2 us
  transfers between devices with their start and end apart: 2, of which 1 were waited for; matrix products, arithmetic and copies ran while one was open for 2% of the time, Pallas kernels for 0%

profile of v1, /device:TPU:0, one launch (start us, length us, event | category | flops | bytes accessed | tf_op | source)
XLA Modules:
  0.0 2181.4 jit_solution(8407940999646100742)
XLA Ops:
  7.2 0.0 copy-start
  7.2 1.4 fusion.21
  8.5 0.1 copy.36
  8.6 0.1 mul.42
  8.8 44.0 %copy.37 = bf16[32,1536,300]{2,1,0:T(8,128)(2,1)} copy(bf16[32,1536,300]{1,0,2:T(8,128)(2,1)} %param.9) | data formatting | bytes 58982400 | tf_op args[0]
  52.7 25.6 %broadcast_multiply_fusion = bf16[32,1536,300]{2,1,0:T(8,128)(2,1)} fusion(bf16[32,1536,300]{2,1,0:T(8,128)(2,1)} %copy.37, bf16[32,1536]{1,0:T(8,128)(2,1)S(1)} %bitcast.64), kind=kLoop, calls=%fused_computation.8 | loop fusion | flops 14745600 | bytes 59080704 | tf_op jit(solution)/shard_map/mul | solution.py:37
  78.3 5.0 fusion.13
  83.3 5.0 fusion.12
  88.3 4.9 fusion.11
  93.2 4.9 fusion.10
  98.2 5.0 fusion.9
  103.1 5.0 fusion.8
  108.1 4.9 fusion.7
  113.1 4.9 fusion.6
  118.0 826.2 %all_to_all.14 = bf16[8,32,192,300]{3,2,1,0:T(8,128)(2,1)} all-to-all(bf16[8,32,192,300]{3,2,1,0:T(8,128)(2,1)} %fusion.6), channel_id=1, replica_groups=mesh['tile'=8,'grp'=4] {'tile'}, dimensions={0} | all-to-all | bytes 58982400 | tf_op jit(solution)/shard_map/all_to_all | solution.py:22
  944.2 0.0 copy-done.1
  944.2 38.2 %convert_bitcast_fusion.1 = bf16[256,192,300]{0,2,1:T(8,128)(2,1)} fusion(bf16[256,192,300]{2,1,0:T(8,128)(2,1)} %bitcast.60, bf16[256,256]{1,0:T(8,128)(2,1)S(1)} %copy-done.1), kind=kOutput, calls=%fused_computation.7 | convolution fusion | flops 7564492800 | bytes 59113472 | tf_op jit(solution)/shard_map/bd,drc->brc/dot_general | solution.py:40
  982.4 45.9 %copy.41 = bf16[256,192,300]{2,1,0:T(8,128)(2,1)} copy(bf16[256,192,300]{0,2,1:T(8,128)(2,1)} %convert_bitcast_fusion.1) | data formatting | bytes 58982400 | tf_op jit(solution)/shard_map/convert_element_type | solution.py:45
  1028.3 7.5 all-to-all-start.1
  1035.7 0.0 copy-start.5
  1035.8 0.0 copy-start.2
  1035.8 0.0 copy-start.3
  1035.8 0.0 copy-start.4
  1035.8 0.0 copy-start.6
  1035.8 0.3 all-reduce.2.cloned.1.call-start
  1036.1 37.0 %fusion.14 = f32[300,300]{1,0:T(8,128)} fusion(bf16[32,1536,300]{2,1,0:T(8,128)(2,1)} %broadcast_multiply_fusion, bf16[32,1536,300]{1,0,2:T(8,128)(2,1)} %param.10), kind=kOutput, calls=%fused_computation.25 | convolution fusion | flops 8847360000 | bytes 59342400 | tf_op jit(solution)/shard_map/dot_general | solution.py:58
  1073.1 0.0 all-reduce.2.cloned.1.call-update
  1073.1 0.0 copy-done.5
  1073.1 0.1 copy.46
  1073.2 0.1 mul.49
  1073.3 0.1 copy.57
  1073.4 0.0 copy-done.2
  1073.4 0.3 copy.44
  1073.7 0.0 copy-done.3
  1073.7 16.7 all_gather.3
  1090.4 3.2 gather_fusion
  1093.6 0.3 convert_bitcast_fusion.2
  1093.9 0.2 copy.45
  1094.1 0.0 copy-done.6
  1094.2 1.3 fusion.17
  1095.4 821.7 %all-reduce.2.cloned.1.call-done = f32[300,300]{1,0:T(8,128)} async-done(((f32[300,300]{1,0:T(8,128)}), f32[300,300]{1,0:T(8,128)}) %all-reduce.2.cloned.1.call-update) | async-done | bytes 360016 | tf_op jit(solution)/shard_map/psum | solution.py:71
  1917.1 1.8 broadcast_multiply_fusion.1
  1919.0 0.0 all-to-all-done.1
  1919.0 36.0 %convert_bitcast_fusion = f32[32,8,192,300]{3,2,0,1:T(8,128)} fusion(bf16[8,32,192,300]{3,2,1,0:T(8,128)(2,1)} %bitcast.16), kind=kLoop, calls=%fused_computation.1 | loop fusion | flops 14745600 | bytes 88473600 | tf_op jit(solution)/shard_map/convert_element_type | solution.py:64
  1955.0 90.5 %copy.54 = f32[32,8,192,300]{2,1,3,0:T(8,128)} copy(f32[32,8,192,300]{3,2,0,1:T(8,128)} %convert_bitcast_fusion) | data formatting | bytes 117964800 | tf_op jit(solution)/shard_map/convert_element_type | solution.py:64
  2045.5 64.1 %reshape.71 = f32[32,1536,300]{1,2,0:T(8,128)} reshape(f32[32,8,192,300]{2,1,3,0:T(8,128)} %copy.54) | data formatting | bytes 117964800 | tf_op jit(solution)/shard_map/convert_element_type | solution.py:64
  2109.7 44.2 %multiply_convert_fusion = bf16[32,1536,300]{1,2,0:T(8,128)(2,1)} fusion(f32[32,1536,300]{1,2,0:T(8,128)} %reshape.71, bf16[32,1536,300]{2,1,0:T(8,128)(2,1)} %broadcast_multiply_fusion, f32[32,1536]{1,0:T(8,128)S(1)} %bitcast.62, f32[1536,300]{0,1:T(8,128)S(1)} %fusion.17, f32[32,1536]{1,0:T(8,128)S(1)} %copy.45, bf16[300,300]{1,0:T(8,128)(2,1)S(1)} %copy-done), kind=kOutput, calls=%fused_computation.2 | convolution fusion | flops 8921088000 | bytes 120381216 | tf_op jit(solution)/shard_map/dot_general | solution.py:55
  2153.9 20.6 copy.49
  (7 shorter events, 0.0 us)
Async XLA Ops:
  7.2 2102.5 %copy-start = (bf16[300,300]{1,0:T(8,128)(2,1)S(1)}, bf16[300,300]{1,0:T(8,128)(2,1)}, u32[]{:S(2)}) copy-start(bf16[300,300]{1,0:T(8,128)(2,1)} %param.12) | copy-start | bytes 540004
  118.0 826.2 %copy-start.1 = (bf16[256,256]{1,0:T(8,128)(2,1)S(1)}, bf16[256,256]{1,0:T(8,128)(2,1)}, u32[]{:S(2)}) copy-start(bf16[256,256]{1,0:T(8,128)(2,1)} %param.13) | copy-start | bytes 393220
  1028.3 890.7 %all-to-all-start.1 = ((bf16[256,192,300]{2,1,0:T(8,128)(2,1)}), bf16[256,192,300]{2,1,0:T(8,128)(2,1)}, u32[]{:S(2)}, u32[]{:S(2)}) async-start(bf16[256,192,300]{2,1,0:T(8,128)(2,1)} %copy.41), calls=%async_computation.1 | async-start | bytes 75497472 | tf_op jit(solution)/shard_map/all_to_all | solution.py:46
  1035.7 37.4 %copy-start.5 = (f32[32,6]{0,1:T(8,128)S(1)}, f32[32,6]{0,1:T(8,128)}, u32[]{:S(2)}) copy-start(f32[32,6]{0,1:T(8,128)} %get-tuple-element.8) | copy-start | bytes 2308
  1035.8 37.6 %copy-start.2 = (bf16[32,2048]{1,0:T(8,128)(2,1)S(1)}, bf16[32,2048]{1,0:T(8,128)(2,1)}, u32[]{:S(2)}) copy-start(bf16[32,2048]{1,0:T(8,128)(2,1)} %param.14) | copy-start | bytes 393220
  1035.8 37.9 %copy-start.3 = (s32[1536]{0:T(1024)S(1)}, s32[1536]{0:T(1024)}, u32[]{:S(2)}) copy-start(s32[1536]{0:T(1024)} %param.16) | copy-start | bytes 18436
  1035.8 58.4 %copy-start.4 = (bf16[30,300]{1,0:T(8,128)(2,1)S(1)}, bf16[30,300]{1,0:T(8,128)(2,1)}, u32[]{:S(2)}) copy-start(bf16[30,300]{1,0:T(8,128)(2,1)} %param.15) | copy-start | bytes 54004
  1035.8 58.4 %copy-start.6 = (s32[1536]{0:T(1024)S(1)}, s32[1536]{0:T(1024)}, u32[]{:S(2)}) copy-start(s32[1536]{0:T(1024)} %param.17) | copy-start | bytes 18436
  1035.8 881.3 %all-reduce.2.cloned.1.call-start = ((), (), s32[]{:S(2)}) async-start(), calls=%async_computation.2 | async-start | bytes 933888 | tf_op jit(solution)/shard_map/psum | solution.py:71
Sparse Core Ops, SparseCore 0:
  1073.2 843.8 all-reduce.1
